TPU v7x, 32 devices: a whole 2x2x4 slice. The times are simulated.
32 devices in a mesh: seq: 8 (over y, x, core), dp: 4 (over z).
Axes of the slice: x: 2, y: 2, z: 4, core: 2. Of those that a mesh axis runs over, the one named last changes fastest.
Arguments:
- tokens: bfloat16 [16384, 1024], P(('dp', 'seq')), parts along dimension 0, may hold values from -6 to 6
- norm_gain: float32 [1024], replicated, may hold values from 0.25 to 1.75
- query_weight: bfloat16 [1024, 1024], replicated
- key_weight: bfloat16 [1024, 1024], replicated
- value_weight: bfloat16 [1024, 1024], replicated, may hold values from -0.1875 to 0.1875
- out_weight: bfloat16 [1024, 1024], replicated, may hold values from -0.1875 to 0.1875
- random_blocks: int32 [256, 3], P('dp'), parts along dimension 0, may hold values from 0 to 63, as said below
- bucket_id: int32 [1], replicated, may hold values from 0 to 7
- global_positions: int32 [8, 128], replicated, may hold values from 0 to 4095, as said below
Outputs:
- layer_out: bfloat16 [16384, 1024], P(('dp', 'seq')), parts along dimension 0
There are 4 independent parts, one for each index of `dp`. A program takes and returns all parts, laid end to end along the dimension named above; an argument that names none is the same for every part. Nothing has to cross between parts.
Inputs may be any that keep to these rules, and one draw needn't show every extreme that they name: `random_blocks`: each row lists 3 block numbers. For the query blocks of one device (aligned runs of 8 rows) at most 3 of the listed blocks lie within the tokens of any one device, and exactly 3 for some device. A block may be listed more than once. `global_positions`: each row holds 128 distinct positions in rising order.
All inputs are finite; a program needn't handle non-finite values.
Results may differ from a plain program's by a relative error of at most 0.0089.
Values may be sent and summed in bfloat16 or wider, within the bound.
No kernel may reach another device: no remote copies, remote signals or barrier semaphores. Data moves between devices by JAX's collectives and lax.ppermute only.
A program may use at most 128 MiB of HBM per device.

v0:
```python
import jax
import jax.numpy as jnp
from jax import lax
from jax.sharding import PartitionSpec as P

HEADS = 16
HDIM = 64
BLOCK = 64
RAND = 3
NGLOB = 128


def with_halo(block, sides, width):
    for axis, dim in sides:
        count = lax.axis_size(axis)
        forward = [(i, i + 1) for i in range(count - 1)]
        forward.append((count - 1, 0))
        backward = [(target, source) for source, target in forward]
        low = lax.ppermute(
            lax.slice_in_dim(block, block.shape[dim] - width, None, axis=dim), axis, forward
        )
        high = lax.ppermute(lax.slice_in_dim(block, 0, width, axis=dim), axis, backward)
        block = jnp.concatenate([low, block, high], axis=dim)
    return block


def combined_all(value, axis, join):
    pieces = jax.tree.map(lambda part: lax.all_gather(part, axis), value)
    head = jax.tree.map(lambda part: part[0], pieces)
    tail = jax.tree.map(lambda part: part[1:], pieces)
    running, _ = lax.scan(lambda running, piece: (join(running, piece), None), head, tail)
    return running


def layer_norm(tokens, norm_gain):
    values = tokens.astype(jnp.float32)
    center = values - jnp.mean(values, axis=-1, keepdims=True)
    spread = jnp.mean(center * center, axis=-1, keepdims=True)
    return (center * lax.rsqrt(spread + 1e-05) * norm_gain).astype(jnp.bfloat16)


def combine_rows(first, second):
    top_score = jnp.maximum(first[0], second[0])
    first_factor = jnp.exp(first[0] - top_score)
    second_factor = jnp.exp(second[0] - top_score)
    total = first[1] * first_factor + second[1] * second_factor
    weighted = first[2] * first_factor[..., None] + second[2] * second_factor[..., None]
    return (top_score, total, weighted)


def body(
    tokens,
    norm_gain,
    query_weight,
    key_weight,
    value_weight,
    out_weight,
    random_blocks,
    bucket_id,
    global_positions,
):
    shards = lax.axis_size("seq")
    device = lax.axis_index("seq")
    rows_here = tokens.shape[0]
    width = tokens.shape[1]
    local_blocks = rows_here // BLOCK
    slots = local_blocks * RAND
    capacity = (slots + shards - 1) // shards
    scale = HDIM ** (-0.5)
    normed = layer_norm(tokens, norm_gain)
    queries = jnp.dot(normed, query_weight, preferred_element_type=jnp.float32).astype(jnp.bfloat16)
    key_rows = jnp.dot(normed, key_weight, preferred_element_type=jnp.float32).astype(jnp.bfloat16)
    value_rows = jnp.dot(normed, value_weight, preferred_element_type=jnp.float32).astype(
        jnp.bfloat16
    )
    paired = jnp.concatenate([key_rows, value_rows], axis=1)
    widened = with_halo(paired, (("seq", 0),), BLOCK)
    wide_blocks = widened.reshape(local_blocks + 2, BLOCK, 2 * width)
    window = jnp.stack([wide_blocks[:-2], wide_blocks[1:-1], wide_blocks[2:]], axis=1)
    window = window.reshape(local_blocks, 3 * BLOCK, 2 * width)
    table = random_blocks.reshape(shards, slots)
    my_table = lax.dynamic_slice_in_dim(table, device, 1, 0)[0]
    source = table // local_blocks
    inner = table % local_blocks
    match = (source == device).astype(jnp.int32)
    rank = jnp.cumsum(match, axis=1) - 1
    slot_iota = jnp.arange(capacity, dtype=jnp.int32)
    select = (match[:, :, None] == 1) & (rank[:, :, None] == slot_iota[None, None, :])
    send_index = jnp.sum(jnp.where(select, inner[:, :, None], 0), axis=1)
    blocks_here = paired.reshape(local_blocks, BLOCK, 2 * width)
    outgoing = blocks_here[send_index]
    incoming = lax.all_to_all(outgoing, "seq", split_axis=0, concat_axis=0, tiled=True)
    incoming = incoming.reshape(shards * capacity, BLOCK, 2 * width)
    my_source = my_table // local_blocks
    slot_order = jnp.arange(slots, dtype=jnp.int32)
    same = (my_source[:, None] == my_source[None, :]) & (slot_order[None, :] < slot_order[:, None])
    my_rank = jnp.sum(same.astype(jnp.int32), axis=1)
    random_rows = incoming[my_source * capacity + my_rank]
    random_rows = random_rows.reshape(local_blocks, RAND * BLOCK, 2 * width)
    positions = global_positions[bucket_id[0]]
    local_position = positions - device * rows_here
    selector = (local_position[:, None] == jnp.arange(rows_here, dtype=jnp.int32)[None, :]).astype(
        jnp.bfloat16
    )
    global_normed = lax.psum(
        jnp.dot(selector, normed, preferred_element_type=jnp.float32).astype(jnp.bfloat16), "seq"
    )
    global_queries = jnp.dot(
        global_normed, query_weight, preferred_element_type=jnp.float32
    ).astype(jnp.bfloat16)
    global_keys = jnp.dot(global_normed, key_weight, preferred_element_type=jnp.float32).astype(
        jnp.bfloat16
    )
    global_values = jnp.dot(global_normed, value_weight, preferred_element_type=jnp.float32).astype(
        jnp.bfloat16
    )
    global_paired = jnp.concatenate([global_keys, global_values], axis=1)
    global_broad = jnp.broadcast_to(global_paired[None], (local_blocks, NGLOB, 2 * width))
    key_set = jnp.concatenate([window, random_rows, global_broad], axis=1)
    count = key_set.shape[1]
    key_part = key_set[:, :, :width].reshape(local_blocks, count, HEADS, HDIM)
    value_part = key_set[:, :, width:].reshape(local_blocks, count, HEADS, HDIM)
    query_blocks = queries.reshape(local_blocks, BLOCK, HEADS, HDIM)
    scores = (
        jnp.einsum("bqhd,bkhd->bhqk", query_blocks, key_part, preferred_element_type=jnp.float32)
        * scale
    )
    top_score = jnp.max(scores, axis=-1, keepdims=True)
    expo = jnp.exp(scores - top_score)
    probs = (expo / jnp.sum(expo, axis=-1, keepdims=True)).astype(jnp.bfloat16)
    sparse_out = jnp.einsum(
        "bhqk,bkhd->bqhd", probs, value_part, preferred_element_type=jnp.float32
    )
    sparse_out = sparse_out.reshape(rows_here, width).astype(jnp.bfloat16)
    global_heads = global_queries.reshape(NGLOB, HEADS, HDIM)
    local_keys = key_rows.reshape(rows_here, HEADS, HDIM)
    local_values = value_rows.astype(jnp.float32).reshape(rows_here, HEADS, HDIM)
    global_scores = (
        jnp.einsum("qhd,khd->hqk", global_heads, local_keys, preferred_element_type=jnp.float32)
        * scale
    )
    global_top = jnp.max(global_scores, axis=-1)
    global_expo = jnp.exp(global_scores - global_top[..., None])
    global_total = jnp.sum(global_expo, axis=-1)
    global_weighted = jnp.einsum(
        "hqk,khd->hqd", global_expo, local_values, precision=lax.Precision.HIGHEST
    )
    merged = combined_all((global_top, global_total, global_weighted), "seq", combine_rows)
    global_out = merged[2] / merged[1][..., None]
    global_out = jnp.transpose(global_out, (1, 0, 2)).reshape(NGLOB, width).astype(jnp.bfloat16)
    placed = jnp.dot(selector.T, global_out, preferred_element_type=jnp.float32).astype(
        jnp.bfloat16
    )
    owned_row = jnp.sum(selector.astype(jnp.float32), axis=0) > 0.5
    mixed = jnp.where(owned_row[:, None], placed, sparse_out)
    return jnp.dot(mixed, out_weight, preferred_element_type=jnp.float32).astype(jnp.bfloat16)


def solution(mesh):
    placed = (P(("dp", "seq"), None), P(), P(), P(), P(), P(), P("dp", None), P(), P())
    return jax.shard_map(
        body, mesh=mesh, in_specs=placed, out_specs=P(("dp", "seq"), None), check_vma=False
    )
```

profile of v0, /device:TPU:0, one launch (start us, length us, event | category | flops | bytes accessed | tf_op | source)
XLA Modules:
  0.0 269.2 jit_solution(3711062153873412040)
XLA Ops:
  6.5 1.6 convert_reduce_fusion
  8.1 1.6 fusion.15
  9.8 3.1 %convolution_convert_fusion.4 = bf16[512,1024]{1,0:T(8,128)(2,1)S(1)} fusion(bf16[1024,1024]{1,0:T(8,128)(2,1)} %param.14, bf16[512,1024]{1,0:T(8,128)(2,1)S(1)} %copy-done.7, f32[1024]{0:T(1024)S(1)} %copy-done.16, f32[512]{0:T(512)S(1)} %add_rsqrt_fusion, f32[512]{0:T(512)S(1)} %broadcast_multiply_fusion), kind=kOutput, calls=%fused_computation.51 | convolution fusion | flops 1076887552 | bytes 4202496 | tf_op jit(solution)/shard_map/dot_general | solution.py:72
  12.9 1.3 convolution_convert_fusion.3
  15.6 2.9 %collective-permute-start.1 = (bf16[64,2048]{1,0:T(8,128)(2,1)}, bf16[64,2048]{1,0:T(8,128)(2,1)}, u32[]{:S(2)}, u32[]{:S(2)}) collective-permute-start(bf16[64,2048]{1,0:T(8,128)(2,1)} %get-tuple-element.99), channel_id=1, source_target_pairs={{4,0},{8,4},{12,8},{16,12},{20,16},{24,20},{28,24},{0,28},{5,1},{9... | collective-permute-start | bytes 786440 | tf_op jit(solution)/shard_map/ppermute | solution.py:22
  19.2 3.7 %collective-permute-done = bf16[64,2048]{1,0:T(8,128)(2,1)S(1)} collective-permute-done((bf16[64,2048]{1,0:T(8,128)(2,1)}, bf16[64,2048]{1,0:T(8,128)(2,1)S(1)}, u32[]{:S(2)}, u32[]{:S(2)}) %collective-permute-start) | collective-permute-done | bytes 262176 | tf_op jit(solution)/shard_map/ppermute | solution.py:19
  22.8 1.6 collective-permute-done.1
  24.5 6.7 %pad_maximum_fusion.5 = (bf16[512,2048]{1,0:T(8,128)(2,1)}, bf16[512,2048]{1,0:T(8,128)(2,1)}, bf16[512,2048]{1,0:T(8,128)(2,1)}) fusion(bf16[64,2048]{1,0:T(8,128)(2,1)S(1)} %collective-permute-done, bf16[512,1024]{1,0:T(8,128)(2,1)S(1)} %convolution_convert_fusion.3, bf16[512,1024]{1,0:T(8,128)(2,1)} %copy-done.3, bf16[64,2048]{1,0:T(8,128)(2,1)} %collective-permute-done.1), kind=kLoop, calls=%fused_computation.39 | loop fusion | flops 16777216 | bytes 8912896 | tf_op jit(solution)/shard_map/concatenate | solution.py:23
  31.2 6.0 %gather_fusion = bf16[24,64,2048]{2,1,0:T(8,128)(2,1)} fusion(bf16[8,64,2048]{2,1,0:T(8,128)(2,1)} %bitcast.101, s32[1024]{0:T(1024)S(1)} %pad_clamp_fusion.1), kind=kCustom, calls=%fused_computation | custom fusion | bytes 12583008 | tf_op jit(solution)/shard_map/gather | solution.py:91
  37.2 4.7 %all-to-all-start = ((bf16[8,3,64,2048]{3,2,1,0:T(8,128)(2,1)}), bf16[8,3,64,2048]{3,2,1,0:T(8,128)(2,1)}, u32[]{:S(2)}, u32[]{:S(2)}) async-start(bf16[8,3,64,2048]{3,2,1,0:T(8,128)(2,1)} %bitcast.104), calls=%async_computation | async-start | bytes 12582912 | tf_op jit(solution)/shard_map/all_to_all | solution.py:92
  43.4 2.5 convolution_convert_fusion.8
  46.3 3.5 %convolution_convert_fusion.2 = bf16[512,1024]{1,0:T(8,128)(2,1)} fusion(bf16[1024,1024]{1,0:T(8,128)(2,1)S(1)} %copy-done, bf16[512,1024]{1,0:T(8,128)(2,1)} %param.11, f32[1024]{0:T(1024)S(1)} %copy-done.16, f32[512]{0:T(512)S(1)} %add_rsqrt_fusion, f32[512]{0:T(512)S(1)} %broadcast_multiply_fusion), kind=kOutput, calls=%fused_computation.49 | convolution fusion | flops 1076887552 | bytes 4202496 | tf_op jit(solution)/shard_map/dot_general | solution.py:71
  49.9 2.3 copy.50
  52.2 1.3 copy.51
  53.5 4.0 %reshape.283 = bf16[8,64,16,64]{3,2,1,0:T(8,128)(2,1)} reshape(bf16[512,1024]{1,0:T(8,128)(2,1)} %convolution_convert_fusion.2) | data formatting | bytes 2097152 | tf_op jit(solution)/shard_map/reshape | solution.py:123
  57.5 71.0 %all-reduce.2.cloned.1.call-done = bf16[128,1024]{1,0:T(8,128)(2,1)} async-done(((bf16[128,1024]{1,0:T(8,128)(2,1)}), bf16[128,1024]{1,0:T(8,128)(2,1)}) %all-reduce.2.cloned.1.call-update) | async-done | bytes 262160 | tf_op jit(solution)/shard_map/psum | solution.py:105
  128.4 1.4 convolution_convert_fusion.7
  130.9 1.2 fusion.10
  132.1 8.7 %all-gather.1 = f32[128,128]{1,0:T(8,128)S(1)} all-gather(f32[16,128]{1,0:T(8,128)S(1)} %fusion.10), channel_id=3, replica_groups=mesh['seq'=8,'dp'=4] {'seq'}, dimensions={0}, use_global_device_ids=true | all-gather | bytes 73728 | tf_op jit(solution)/shard_map/all_gather | solution.py:28
  140.8 8.9 %all-gather = f32[128,128]{1,0:T(8,128)S(1)} all-gather(f32[16,128]{1,0:T(8,128)S(1)} %get-tuple-element.102), channel_id=2, replica_groups=mesh['seq'=8,'dp'=4] {'seq'}, dimensions={0}, use_global_device_ids=true | all-gather | bytes 73728 | tf_op jit(solution)/shard_map/all_gather | solution.py:28
  149.8 4.0 %fusion.9 = f32[16,128,64]{1,2,0:T(8,128)} fusion(bf16[512,16,64]{0,2,1:T(8,128)(2,1)S(1)} %bitcast.111, f32[16,128,512]{2,1,0:T(8,128)S(1)} %get-tuple-element.103, f32[16,128]{1,0:T(8,128)S(1)} %get-tuple-element.102), kind=kOutput, calls=%fused_computation.22 | convolution fusion | flops 807403520 | bytes 5775360 | tf_op jit(solution)/shard_map/hqk,khd->hqd/dot_general | solution.py:145
  153.8 2.2 convolution_convert_fusion.5
  156.0 2.2 convolution_convert_fusion.6
  158.4 3.3 %pad_maximum_fusion.1 = bf16[8,3,64,2048]{3,2,1,0:T(8,128)(2,1)} fusion(bf16[8,1,64,2048]{3,2,1,0:T(8,128)(2,1)S(1)} %bitcast.110, bf16[8,1,64,2048]{3,2,1,0:T(8,128)(2,1)S(1)} %bitcast.102, bf16[8,1,64,2048]{3,2,1,0:T(8,128)(2,1)S(1)} %bitcast.109), kind=kLoop, calls=%fused_computation.19 | loop fusion | flops 6291456 | bytes 12582912 | tf_op jit(solution)/shard_map/stack | solution.py:79
  161.7 7.4 %gather_fusion.1 = bf16[24,64,2048]{2,1,0:T(8,128)(2,1)} fusion(bf16[24,64,2048]{2,1,0:T(8,128)(2,1)} %bitcast.23, s32[1024]{0:T(1024)S(1)} %pad_clamp_fusion), kind=kCustom, calls=%fused_computation.1 | custom fusion | bytes 12583008 | tf_op jit(solution)/shard_map/gather | solution.py:98
  169.6 7.8 %pad_maximum_fusion = bf16[8,512,2048]{2,1,0:T(8,128)(2,1)S(1)} fusion(bf16[8,128,2048]{2,1,0:T(8,128)(2,1)S(1)} %broadcast_in_dim.22, bf16[8,192,2048]{2,1,0:T(8,128)(2,1)} %bitcast.106, bf16[8,192,2048]{2,1,0:T(8,128)(2,1)} %bitcast.105), kind=kLoop, calls=%fused_computation.12 | loop fusion | flops 50331648 | bytes 33554432 | tf_op jit(solution)/shard_map/concatenate | solution.py:119
  177.3 6.3 %fusion.53 = (bf16[8,512,1024]{2,1,0:T(8,128)(2,1)}, bf16[8,512,1024]{2,1,0:T(8,128)(2,1)}) fusion(bf16[8,512,2048]{2,1,0:T(8,128)(2,1)S(1)} %pad_maximum_fusion), kind=kLoop, calls=%fused_computation.113 | loop fusion | bytes 33554432 | tf_op jit(solution)/shard_map/slice | solution.py:121
  183.6 11.5 %copy.61 = bf16[8,512,1024]{1,2,0:T(8,128)(2,1)} copy(bf16[8,512,1024]{2,1,0:T(8,128)(2,1)} %get-tuple-element.93) | data formatting | bytes 16777216 | tf_op jit(solution)/shard_map/slice | solution.py:121
  195.1 11.6 %copy.60 = bf16[8,512,1024]{1,2,0:T(8,128)(2,1)} copy(bf16[8,512,1024]{2,1,0:T(8,128)(2,1)} %get-tuple-element.94) | data formatting | bytes 16777216 | tf_op jit(solution)/shard_map/slice | solution.py:122
  206.7 10.5 %fusion.54 = (f32[8,16,64]{2,1,0:T(8,128)S(1)}, f32[8,16,64,512]{3,2,1,0:T(8,128)}) fusion(bf16[8,512,16,64]{1,3,2,0:T(8,128)(2,1)} %bitcast.103, bf16[8,64,16,64]{3,2,1,0:T(8,128)(2,1)S(1)} %copy-done.6), kind=kOutput, calls=%fused_computation.114 | convolution fusion | flops 549454336 | bytes 26247168 | tf_op jit(solution)/shard_map/sub | solution.py:129
  217.1 10.9 %convert_bitcast_fusion = bf16[8,64,16,64]{1,3,2,0:T(8,128)(2,1)} fusion(bf16[8,512,16,64]{1,3,2,0:T(8,128)(2,1)} %bitcast.108, f32[8,16,64,512]{3,2,1,0:T(8,128)} %get-tuple-element.101, f32[8,16,64]{2,1,0:T(8,128)S(1)} %get-tuple-element.100), kind=kOutput, calls=%fused_computation.41 | convolution fusion | flops 545783808 | bytes 26247168 | tf_op jit(solution)/shard_map/bhqk,bkhd->bqhd/dot_general | solution.py:131
  228.1 3.6 %copy.63 = bf16[8,64,16,64]{3,2,1,0:T(8,128)(2,1)S(1)} copy(bf16[8,64,16,64]{1,3,2,0:T(8,128)(2,1)} %convert_bitcast_fusion) | data formatting | bytes 2097152 | tf_op jit(solution)/shard_map/convert_element_type | solution.py:134
  231.7 2.3 convert_element_type.95
  234.0 1.1 slice.66
  235.4 4.3 %slice.69 = f32[112,128,64]{1,2,0:T(8,128)} slice(f32[128,128,64]{1,2,0:T(8,128)} %all-gather.5.cloned.1.call-done), slice={[16:128], [0:128], [0:64]} | slice | bytes 7340032 | tf_op jit(solution)/shard_map/slice | solution.py:30
  239.8 17.1 %while.14 = (s32[]{:T(128)}, f32[16,128]{1,0:T(8,128)S(1)}, f32[16,128]{1,0:T(8,128)S(1)}, f32[16,128,64]{2,1,0:T(8,128)S(1)}, f32[7,16,128]{2,1,0:T(8,128)S(1)}...) while((s32[]{:T(128)}, f32[16,128]{1,0:T(8,128)S(1)}, f32[16,128]{1,0:T(8,128)S(1)}, ...), condition=%wide.region_7.8_spmd, body=%wide.region_6.7_spmd.sunk | while | flops 405506 | bytes 3752029 | solution.py:31
  239.8 1.1 constant_dynamic-slice_fusion.3
  241.2 1.0 fusion.79
  242.2 1.1 constant_dynamic-slice_fusion.3
  243.7 1.0 fusion.79
  244.7 1.1 constant_dynamic-slice_fusion.3
  247.1 1.1 constant_dynamic-slice_fusion.3
  249.6 1.1 constant_dynamic-slice_fusion.3
  252.0 1.1 constant_dynamic-slice_fusion.3
  253.4 1.0 fusion.79
  254.5 1.1 constant_dynamic-slice_fusion.3
  255.9 1.0 fusion.79
  258.1 4.2 %convolution_convert_fusion.1 = bf16[512,1024]{1,0:T(8,128)(2,1)} fusion(bf16[1024,1024]{1,0:T(8,128)(2,1)} %param.16, bf16[512,1024]{1,0:T(8,128)(2,1)S(1)} %copy-done.12, bf16[128,1024]{0,1:T(8,128)(2,1)S(1)} %bitcast.114, pred[512]{0:T(512)(128)(4,1)S(1)} %broadcast_compare_fusion.1, s32[128]{0:T(128)S(1)} %subtract_bitcast_fusion), kind=kOutput, calls=%fused_computation.48 | convolution fusion | flops 1209663488 | bytes 4457472 | tf_op jit(solution)/shard_map/dot_general | solution.py:156
  (92 shorter events, 11.8 us)
Async XLA Ops:
  6.5 39.8 %copy-start = (bf16[1024,1024]{1,0:T(8,128)(2,1)S(1)}, bf16[1024,1024]{1,0:T(8,128)(2,1)}, u32[]{:S(2)}) copy-start(bf16[1024,1024]{1,0:T(8,128)(2,1)} %param.13) | copy-start | bytes 6291460
  6.5 3.2 %copy-start.7 = (bf16[512,1024]{1,0:T(8,128)(2,1)S(1)}, bf16[512,1024]{1,0:T(8,128)(2,1)}, u32[]{:S(2)}) copy-start(bf16[512,1024]{1,0:T(8,128)(2,1)} %param.11) | copy-start | bytes 3145732
  6.5 3.3 %copy-start.16 = (f32[1024]{0:T(1024)S(1)}, f32[1024]{0:T(1024)}, u32[]{:S(2)}) copy-start(f32[1024]{0:T(1024)} %param.12) | copy-start | bytes 12292
  9.8 3.1 %copy-start.11 = (bf16[1024,1024]{1,0:T(8,128)(2,1)S(1)}, bf16[1024,1024]{1,0:T(8,128)(2,1)}, u32[]{:S(2)}) copy-start(bf16[1024,1024]{1,0:T(8,128)(2,1)} %param.15) | copy-start | bytes 6291460
  12.9 1.4 copy-start.3
  14.3 4.2 %copy-start.15 = (s32[64,3]{0,1:T(4,128)S(1)}, s32[64,3]{0,1:T(4,128)}, u32[]{:S(2)}) copy-start(s32[64,3]{0,1:T(4,128)} %param.17) | copy-start | bytes 2308
  15.1 7.7 %collective-permute-start = (bf16[64,2048]{1,0:T(8,128)(2,1)}, bf16[64,2048]{1,0:T(8,128)(2,1)S(1)}, u32[]{:S(2)}, u32[]{:S(2)}) collective-permute-start(bf16[64,2048]{1,0:T(8,128)(2,1)} %get-tuple-element.98), channel_id=1, source_target_pairs={{0,4},{4,8},{8,12},{12,16},{16,20},{20,24},{24,28},{28,0},{1,5},{5... | collective-permute-start | bytes 786440 | tf_op jit(solution)/shard_map/ppermute | solution.py:19
  15.6 8.9 %collective-permute-start.1 = (bf16[64,2048]{1,0:T(8,128)(2,1)}, bf16[64,2048]{1,0:T(8,128)(2,1)}, u32[]{:S(2)}, u32[]{:S(2)}) collective-permute-start(bf16[64,2048]{1,0:T(8,128)(2,1)} %get-tuple-element.99), channel_id=1, source_target_pairs={{4,0},{8,4},{12,8},{16,12},{20,16},{24,20},{28,24},{0,28},{5,1},{9... | collective-permute-start | bytes 786440 | tf_op jit(solution)/shard_map/ppermute | solution.py:22
  37.2 124.4 %all-to-all-start = ((bf16[8,3,64,2048]{3,2,1,0:T(8,128)(2,1)}), bf16[8,3,64,2048]{3,2,1,0:T(8,128)(2,1)}, u32[]{:S(2)}, u32[]{:S(2)}) async-start(bf16[8,3,64,2048]{3,2,1,0:T(8,128)(2,1)} %bitcast.104), calls=%async_computation | async-start | bytes 12582912 | tf_op jit(solution)/shard_map/all_to_all | solution.py:92
  42.0 86.5 %all-reduce.2.cloned.1.call-start = ((), (), s32[]{:S(2)}) async-start(), calls=%async_computation.1 | async-start | bytes 524288 | tf_op jit(solution)/shard_map/psum | solution.py:105
  45.9 188.0 %all-gather.5.cloned.1.call-start = ((), (), s32[]{:S(2)}) async-start(), calls=%async_computation.2 | async-start | bytes 4718592 | tf_op jit(solution)/shard_map/all_gather | solution.py:28
  57.5 72.5 %copy-start.9 = (bf16[512,1024]{0,1:T(8,128)(2,1)S(1)}, bf16[512,1024]{0,1:T(8,128)(2,1)}, u32[]{:S(2)}) copy-start(bf16[512,1024]{0,1:T(8,128)(2,1)} %copy.50) | copy-start | bytes 3145732
  130.9 18.9 %copy-start.8 = (bf16[512,1024]{0,1:T(8,128)(2,1)S(1)}, bf16[512,1024]{0,1:T(8,128)(2,1)}, u32[]{:S(2)}) copy-start(bf16[512,1024]{0,1:T(8,128)(2,1)} %copy.51) | copy-start | bytes 3145732
  140.8 17.4 %copy-start.13 = (f32[128,128]{1,0:T(8,128)}, f32[128,128]{1,0:T(8,128)S(1)}, u32[]{:S(2)}) copy-start(f32[128,128]{1,0:T(8,128)S(1)} %all-gather.1) | copy-start | bytes 196612
  149.8 8.5 %copy-start.14 = (f32[128,128]{1,0:T(8,128)}, f32[128,128]{1,0:T(8,128)S(1)}, u32[]{:S(2)}) copy-start(f32[128,128]{1,0:T(8,128)S(1)} %all-gather) | copy-start | bytes 196612
  149.8 4.0 %copy-start.10 = (bf16[128,1024]{1,0:T(8,128)(2,1)S(1)}, bf16[128,1024]{1,0:T(8,128)(2,1)}, u32[]{:S(2)}) copy-start(bf16[128,1024]{1,0:T(8,128)(2,1)} %all-reduce.2.cloned.1.call-done) | copy-start | bytes 786436
  153.8 4.5 %copy-start.4 = (bf16[512,2048]{1,0:T(8,128)(2,1)S(1)}, bf16[512,2048]{1,0:T(8,128)(2,1)}, u32[]{:S(2)}) copy-start(bf16[512,2048]{1,0:T(8,128)(2,1)} %get-tuple-element.95) | copy-start | bytes 6291460
  153.8 4.5 %copy-start.5 = (bf16[512,2048]{1,0:T(8,128)(2,1)S(1)}, bf16[512,2048]{1,0:T(8,128)(2,1)}, u32[]{:S(2)}) copy-start(bf16[512,2048]{1,0:T(8,128)(2,1)} %get-tuple-element.96) | copy-start | bytes 6291460
  156.0 2.4 copy-start.2
  195.1 11.6 %copy-start.6 = (bf16[8,64,16,64]{3,2,1,0:T(8,128)(2,1)S(1)}, bf16[8,64,16,64]{3,2,1,0:T(8,128)(2,1)}, u32[]{:S(2)}) copy-start(bf16[8,64,16,64]{3,2,1,0:T(8,128)(2,1)} %reshape.283) | copy-start | bytes 3145732
  235.4 4.4 %slice-start = ((f32[128,128]{1,0:T(8,128)}), f32[16,128]{1,0:T(8,128)S(1)}, s32[]{:S(2)}) async-start(f32[128,128]{1,0:T(8,128)} %copy-done.13), calls=%async_computation.3 | async-start | bytes 16384 | tf_op jit(solution)/shard_map/slice | solution.py:29
  235.4 4.3 %slice-start.1 = ((f32[128,128]{1,0:T(8,128)}), f32[16,128]{1,0:T(8,128)S(1)}, s32[]{:S(2)}) async-start(f32[128,128]{1,0:T(8,128)} %copy-done.14), calls=%async_computation.4 | async-start | bytes 16384 | tf_op jit(solution)/shard_map/slice | solution.py:29
  256.9 1.2 copy-start.12
  257.3 5.1 %copy-start.1 = (bf16[1024,1024]{1,0:T(8,128)(2,1)S(1)}, bf16[1024,1024]{1,0:T(8,128)(2,1)}, u32[]{:S(2)}) copy-start(bf16[1024,1024]{1,0:T(8,128)(2,1)} %param.13) | copy-start | bytes 6291460
Sparse Core Ops, SparseCore 0:
  46.0 82.3 all-reduce.1
  153.9 36.7 all-gather.4
where the time goes:
time: 271 us; the launch traced here: 269 us
  waiting for transfers between devices  76.3 us (28%)
  local copies, waits for them, and re-layouts  74.2 us (27%)
  matrix products  46.6 us (17%)
  other arithmetic  31.5 us (12%)
  blocking collectives  17.6 us (6%)
  between operations  14.4 us (5%)
  starting transfers between devices  8.15 us (3%)
    psum x1, waiting for transfers between devices, body(): lax.psum(jnp.dot(selector, normed, preferred_element_type=jnp.float32).as...  71 us
    slice x2, local copies, waits for them, and re-layouts, body(): key_part = key_set[:, :, :width].reshape(local_blocks, count, HEADS, HDIM)  17.8 us
    all_gather x2, blocking collectives, combined_all(): pieces = jax.tree.map(lambda part: lax.all_gather(part, axis), value)  17.6 us
    slice x1, local copies, waits for them, and re-layouts, body(): value_part = key_set[:, :, width:].reshape(local_blocks, count, HEADS, HDIM)  11.6 us
    dot_general x1, matrix products, body(): jnp.einsum('bhqk,bkhd->bqhd', probs, value_part, preferred_element_type=j...  10.9 us
    sub x1, matrix products, body(): expo = jnp.exp(scores - top_score)  10.5 us
    dynamic_slice x14, local copies, waits for them, and re-layouts, combined_all(): lax.scan(lambda running, piece: (join(running, piece), None), head, tail)  9.93 us
    concatenate x1, other arithmetic, body(): key_set = jnp.concatenate([window, random_rows, global_broad], axis=1)  7.77 us
  transfers between devices with their start and end apart: 5, of which 3 were waited for; matrix products, arithmetic and copies ran while one was open for 38% of the time, Pallas kernels for 0%

commit v1 on v0

--- a/solution.py
+++ b/solution.py
@@ -102,8 +102,12 @@
     selector = (local_position[:, None] == jnp.arange(rows_here, dtype=jnp.int32)[None, :]).astype(
         jnp.bfloat16
     )
-    global_normed = lax.psum(
-        jnp.dot(selector, normed, preferred_element_type=jnp.float32).astype(jnp.bfloat16), "seq"
+    global_normed = jnp.sum(
+        lax.all_gather(
+            jnp.dot(selector, normed, preferred_element_type=jnp.float32).astype(jnp.bfloat16),
+            "seq",
+        ),
+        axis=0,
     )
     global_queries = jnp.dot(
         global_normed, query_weight, preferred_element_type=jnp.float32

time: 271 us -> 247 us (0.911)
  waiting for transfers between devices: 76.3 us -> 8.17 us
  blocking collectives: 17.6 us -> 61.8 us
  matrix products: 46.6 us -> 42.4 us
  other arithmetic: 31.5 us -> 35.7 us
    psum x1 -> x0, waiting for transfers between devices: 71 us -> none  [body(): lax.psum(jnp.dot(selector, normed, preferred_element_type=jnp.float32).as...]
    all_gather x2, blocking collectives: 17.6 us -> 61.8 us  [combined_all(): pieces = jax.tree.map(lambda part: lax.all_gather(part, axis), value)]
    another operation x1, other arithmetic: 3.27 us -> 6.13 us  [body(): jnp.stack([wide_blocks[:-2], wide_blocks[1:-1], wide_blocks[2:]], axis=1)]
    ppermute x1, waiting for transfers between devices: 1.65 us -> 4.45 us  [with_halo(): lax.ppermute(lax.slice_in_dim(block, 0, width, axis=dim), axis, backward)]
  transfers between devices with their start and end apart: 5 -> 5, of which waited for: 3 -> 2; matrix products, arithmetic and copies ran while one was open for 38% -> 48% of each run, Pallas kernels for 0% -> 0%
where the time goes in v1:
time: 247 us; the launch traced here: 245 us
  local copies, waits for them, and re-layouts  73.8 us (30%)
  blocking collectives  61.8 us (25%)
  matrix products  42.4 us (17%)
  other arithmetic  35.7 us (14%)
  between operations  14.5 us (6%)
  starting transfers between devices  8.32 us (3%)
  waiting for transfers between devices  8.17 us (3%)
    all_gather x2, blocking collectives, combined_all(): pieces = jax.tree.map(lambda part: lax.all_gather(part, axis), value)  61.8 us
    slice x2, local copies, waits for them, and re-layouts, body(): key_part = key_set[:, :, :width].reshape(local_blocks, count, HEADS, HDIM)  18 us
    slice x1, local copies, waits for them, and re-layouts, body(): value_part = key_set[:, :, width:].reshape(local_blocks, count, HEADS, HDIM)  11.6 us
    dot_general x1, matrix products, body(): jnp.einsum('bhqk,bkhd->bqhd', probs, value_part, preferred_element_type=j...  10.9 us
    sub x1, matrix products, body(): expo = jnp.exp(scores - top_score)  10.5 us
    dynamic_slice x14, local copies, waits for them, and re-layouts, combined_all(): lax.scan(lambda running, piece: (join(running, piece), None), head, tail)  9.93 us
    gather x1, local copies, waits for them, and re-layouts, body(): random_rows = incoming[my_source * capacity + my_rank]  7.5 us
    concatenate x1, other arithmetic, body(): key_set = jnp.concatenate([window, random_rows, global_broad], axis=1)  7.25 us
  transfers between devices with their start and end apart: 5, of which 2 were waited for; matrix products, arithmetic and copies ran while one was open for 48% of the time, Pallas kernels for 0%

profile of v1, /device:TPU:0, one launch (start us, length us, event | category | flops | bytes accessed | tf_op | source)
XLA Modules:
  0.0 244.9 jit_solution(10250483867918517514)
XLA Ops:
  7.3 1.5 convert_reduce_fusion
  8.9 1.6 fusion.15
  11.2 1.3 convolution_convert_fusion.8
  12.5 3.0 %convolution_convert_fusion.4 = bf16[512,1024]{1,0:T(8,128)(2,1)S(1)} fusion(bf16[1024,1024]{1,0:T(8,128)(2,1)} %param.14, bf16[512,1024]{1,0:T(8,128)(2,1)S(1)} %copy-done.4, f32[1024]{0:T(1024)S(1)} %copy-done.14, f32[512]{0:T(512)S(1)} %add_rsqrt_fusion, f32[512]{0:T(512)S(1)} %broadcast_multiply_fusion), kind=kOutput, calls=%fused_computation.51 | convolution fusion | flops 1076887552 | bytes 4202496 | tf_op jit(solution)/shard_map/dot_general | solution.py:72
  15.6 1.3 convolution_convert_fusion.3
  18.3 2.9 %collective-permute-start.1 = (bf16[64,2048]{1,0:T(8,128)(2,1)}, bf16[64,2048]{1,0:T(8,128)(2,1)}, u32[]{:S(2)}, u32[]{:S(2)}) collective-permute-start(bf16[64,2048]{1,0:T(8,128)(2,1)} %get-tuple-element.99), channel_id=1, source_target_pairs={{4,0},{8,4},{12,8},{16,12},{20,16},{24,20},{28,24},{0,28},{5,1},{9... | collective-permute-start | bytes 786440 | tf_op jit(solution)/shard_map/ppermute | solution.py:22
  21.9 3.7 %collective-permute-done = bf16[64,2048]{1,0:T(8,128)(2,1)S(1)} collective-permute-done((bf16[64,2048]{1,0:T(8,128)(2,1)}, bf16[64,2048]{1,0:T(8,128)(2,1)S(1)}, u32[]{:S(2)}, u32[]{:S(2)}) %collective-permute-start) | collective-permute-done | bytes 262176 | tf_op jit(solution)/shard_map/ppermute | solution.py:19
  25.6 4.4 %collective-permute-done.1 = bf16[64,2048]{1,0:T(8,128)(2,1)} collective-permute-done((bf16[64,2048]{1,0:T(8,128)(2,1)}, bf16[64,2048]{1,0:T(8,128)(2,1)}, u32[]{:S(2)}, u32[]{:S(2)}) %collective-permute-start.1) | collective-permute-done | bytes 262176 | tf_op jit(solution)/shard_map/ppermute | solution.py:22
  30.0 6.7 %pad_maximum_fusion.5 = (bf16[512,2048]{1,0:T(8,128)(2,1)}, bf16[512,2048]{1,0:T(8,128)(2,1)}, bf16[512,2048]{1,0:T(8,128)(2,1)}) fusion(bf16[64,2048]{1,0:T(8,128)(2,1)S(1)} %collective-permute-done, bf16[512,1024]{1,0:T(8,128)(2,1)S(1)} %convolution_convert_fusion.3, bf16[512,1024]{1,0:T(8,128)(2,1)} %copy-done.2, bf16[64,2048]{1,0:T(8,128)(2,1)} %collective-permute-done.1), kind=kLoop, calls=%fused_computation.39 | loop fusion | flops 16777216 | bytes 8912896 | tf_op jit(solution)/shard_map/concatenate | solution.py:23
  36.7 6.1 %gather_fusion = bf16[24,64,2048]{2,1,0:T(8,128)(2,1)} fusion(bf16[8,64,2048]{2,1,0:T(8,128)(2,1)} %bitcast.102, s32[1024]{0:T(1024)S(1)} %pad_clamp_fusion.1), kind=kCustom, calls=%fused_computation | custom fusion | bytes 12583008 | tf_op jit(solution)/shard_map/gather | solution.py:91
  42.8 4.8 %all-to-all-start = ((bf16[8,3,64,2048]{3,2,1,0:T(8,128)(2,1)}), bf16[8,3,64,2048]{3,2,1,0:T(8,128)(2,1)}, u32[]{:S(2)}, u32[]{:S(2)}) async-start(bf16[8,3,64,2048]{3,2,1,0:T(8,128)(2,1)} %bitcast.105), calls=%async_computation | async-start | bytes 12582912 | tf_op jit(solution)/shard_map/all_to_all | solution.py:92
  47.8 2.3 copy.50
  50.1 1.3 copy.51
  51.4 2.5 %convolution_convert_fusion.2 = bf16[512,1024]{1,0:T(8,128)(2,1)S(1)} fusion(bf16[1024,1024]{1,0:T(8,128)(2,1)S(1)} %copy-done, bf16[512,1024]{1,0:T(8,128)(2,1)} %param.11, f32[1024]{0:T(1024)S(1)} %copy-done.14, f32[512]{0:T(512)S(1)} %add_rsqrt_fusion, f32[512]{0:T(512)S(1)} %broadcast_multiply_fusion), kind=kOutput, calls=%fused_computation.49 | convolution fusion | flops 1076887552 | bytes 4202496 | tf_op jit(solution)/shard_map/dot_general | solution.py:71
  53.9 2.3 reshape.283
  56.6 6.1 %pad_maximum_fusion.1 = bf16[8,3,64,2048]{3,2,1,0:T(8,128)(2,1)} fusion(bf16[8,1,64,2048]{3,2,1,0:T(8,128)(2,1)} %bitcast.111, bf16[8,1,64,2048]{3,2,1,0:T(8,128)(2,1)} %bitcast.103, bf16[8,1,64,2048]{3,2,1,0:T(8,128)(2,1)} %bitcast.110), kind=kLoop, calls=%fused_computation.19 | loop fusion | flops 6291456 | bytes 12582912 | tf_op jit(solution)/shard_map/stack | solution.py:79
  62.7 2.0 reduce_sum.82
  64.7 1.1 convolution_convert_fusion.7
  65.8 1.1 copy.49
  67.8 1.2 fusion.10
  69.0 53.5 %all-gather.2 = f32[128,128]{1,0:T(8,128)S(1)} all-gather(f32[16,128]{1,0:T(8,128)S(1)} %fusion.10), channel_id=4, replica_groups=mesh['seq'=8,'dp'=4] {'seq'}, dimensions={0}, use_global_device_ids=true | all-gather | bytes 73728 | tf_op jit(solution)/shard_map/all_gather | solution.py:28
  122.6 8.3 %all-gather.1 = f32[128,128]{1,0:T(8,128)S(1)} all-gather(f32[16,128]{1,0:T(8,128)S(1)} %get-tuple-element.102), channel_id=3, replica_groups=mesh['seq'=8,'dp'=4] {'seq'}, dimensions={0}, use_global_device_ids=true | all-gather | bytes 73728 | tf_op jit(solution)/shard_map/all_gather | solution.py:28
  130.8 4.0 %fusion.9 = f32[16,128,64]{1,2,0:T(8,128)} fusion(bf16[512,16,64]{0,2,1:T(8,128)(2,1)S(1)} %bitcast.112, f32[16,128,512]{2,1,0:T(8,128)S(1)} %get-tuple-element.103, f32[16,128]{1,0:T(8,128)S(1)} %get-tuple-element.102), kind=kOutput, calls=%fused_computation.22 | convolution fusion | flops 807403520 | bytes 5775360 | tf_op jit(solution)/shard_map/hqk,khd->hqd/dot_general | solution.py:149
  134.8 2.2 convolution_convert_fusion.5
  137.6 7.5 %gather_fusion.1 = bf16[24,64,2048]{2,1,0:T(8,128)(2,1)} fusion(bf16[24,64,2048]{2,1,0:T(8,128)(2,1)} %bitcast.24, s32[1024]{0:T(1024)S(1)} %pad_clamp_fusion), kind=kCustom, calls=%fused_computation.1 | custom fusion | bytes 12583008 | tf_op jit(solution)/shard_map/gather | solution.py:98
  145.6 7.3 %pad_maximum_fusion = bf16[8,512,2048]{2,1,0:T(8,128)(2,1)S(1)} fusion(bf16[8,128,2048]{2,1,0:T(8,128)(2,1)S(1)} %broadcast_in_dim.22, bf16[8,192,2048]{2,1,0:T(8,128)(2,1)} %bitcast.107, bf16[8,192,2048]{2,1,0:T(8,128)(2,1)} %bitcast.106), kind=kLoop, calls=%fused_computation.12 | loop fusion | flops 50331648 | bytes 33554432 | tf_op jit(solution)/shard_map/concatenate | solution.py:123
  152.9 6.4 %fusion.53 = (bf16[8,512,1024]{2,1,0:T(8,128)(2,1)}, bf16[8,512,1024]{2,1,0:T(8,128)(2,1)}) fusion(bf16[8,512,2048]{2,1,0:T(8,128)(2,1)S(1)} %pad_maximum_fusion), kind=kLoop, calls=%fused_computation.113 | loop fusion | bytes 33554432 | tf_op jit(solution)/shard_map/slice | solution.py:125
  159.2 11.6 %copy.61 = bf16[8,512,1024]{1,2,0:T(8,128)(2,1)} copy(bf16[8,512,1024]{2,1,0:T(8,128)(2,1)} %get-tuple-element.93) | data formatting | bytes 16777216 | tf_op jit(solution)/shard_map/slice | solution.py:125
  170.8 11.6 %copy.60 = bf16[8,512,1024]{1,2,0:T(8,128)(2,1)} copy(bf16[8,512,1024]{2,1,0:T(8,128)(2,1)} %get-tuple-element.94) | data formatting | bytes 16777216 | tf_op jit(solution)/shard_map/slice | solution.py:126
  182.5 10.5 %fusion.54 = (f32[8,16,64]{2,1,0:T(8,128)S(1)}, f32[8,16,64,512]{3,2,1,0:T(8,128)}) fusion(bf16[8,512,16,64]{1,3,2,0:T(8,128)(2,1)} %bitcast.104, bf16[8,64,16,64]{3,2,1,0:T(8,128)(2,1)S(1)} %copy-done.3), kind=kOutput, calls=%fused_computation.114 | convolution fusion | flops 549454336 | bytes 26247168 | tf_op jit(solution)/shard_map/sub | solution.py:133
  192.9 10.9 %convert_bitcast_fusion = bf16[8,64,16,64]{1,3,2,0:T(8,128)(2,1)} fusion(bf16[8,512,16,64]{1,3,2,0:T(8,128)(2,1)} %bitcast.109, f32[8,16,64,512]{3,2,1,0:T(8,128)} %get-tuple-element.101, f32[8,16,64]{2,1,0:T(8,128)S(1)} %get-tuple-element.100), kind=kOutput, calls=%fused_computation.41 | convolution fusion | flops 545783808 | bytes 26247168 | tf_op jit(solution)/shard_map/bhqk,bkhd->bqhd/dot_general | solution.py:135
  203.8 3.6 %copy.63 = bf16[8,64,16,64]{3,2,1,0:T(8,128)(2,1)S(1)} copy(bf16[8,64,16,64]{1,3,2,0:T(8,128)(2,1)} %convert_bitcast_fusion) | data formatting | bytes 2097152 | tf_op jit(solution)/shard_map/convert_element_type | solution.py:138
  207.5 2.3 convert_element_type.97
  209.7 1.1 slice.66
  211.2 4.3 %slice.69 = f32[112,128,64]{1,2,0:T(8,128)} slice(f32[128,128,64]{1,2,0:T(8,128)} %all-gather.9.cloned.1.call-done), slice={[16:128], [0:128], [0:64]} | slice | bytes 7340032 | tf_op jit(solution)/shard_map/slice | solution.py:30
  215.5 17.1 %while.14 = (s32[]{:T(128)}, f32[16,128]{1,0:T(8,128)S(1)}, f32[16,128]{1,0:T(8,128)S(1)}, f32[16,128,64]{2,1,0:T(8,128)S(1)}, f32[7,16,128]{2,1,0:T(8,128)S(1)}...) while((s32[]{:T(128)}, f32[16,128]{1,0:T(8,128)S(1)}, f32[16,128]{1,0:T(8,128)S(1)}, ...), condition=%wide.region_7.8_spmd, body=%wide.region_6.7_spmd.sunk | while | flops 405506 | bytes 3752029 | solution.py:31
  215.6 1.1 constant_dynamic-slice_fusion.3
  217.0 1.0 fusion.79
  218.0 1.1 constant_dynamic-slice_fusion.3
  219.4 1.0 fusion.79
  220.4 1.1 constant_dynamic-slice_fusion.3
  222.9 1.1 constant_dynamic-slice_fusion.3
  224.3 1.0 fusion.79
  225.3 1.1 constant_dynamic-slice_fusion.3
  226.8 1.0 fusion.79
  227.8 1.1 constant_dynamic-slice_fusion.3
  230.2 1.1 constant_dynamic-slice_fusion.3
  233.9 4.2 %convolution_convert_fusion.1 = bf16[512,1024]{1,0:T(8,128)(2,1)} fusion(bf16[1024,1024]{1,0:T(8,128)(2,1)} %param.16, bf16[512,1024]{1,0:T(8,128)(2,1)S(1)} %copy-done.10, bf16[128,1024]{0,1:T(8,128)(2,1)S(1)} %bitcast.116, pred[512]{0:T(512)(128)(4,1)S(1)} %broadcast_compare_fusion.1, s32[128]{0:T(128)S(1)} %subtract_bitcast_fusion), kind=kOutput, calls=%fused_computation.48 | convolution fusion | flops 1209663488 | bytes 4457472 | tf_op jit(solution)/shard_map/dot_general | solution.py:160
  (89 shorter events, 12.2 us)
Async XLA Ops:
  6.5 44.8 %copy-start = (bf16[1024,1024]{1,0:T(8,128)(2,1)S(1)}, bf16[1024,1024]{1,0:T(8,128)(2,1)}, u32[]{:S(2)}) copy-start(bf16[1024,1024]{1,0:T(8,128)(2,1)} %param.13) | copy-start | bytes 6291460
  6.5 4.7 %copy-start.4 = (bf16[512,1024]{1,0:T(8,128)(2,1)S(1)}, bf16[512,1024]{1,0:T(8,128)(2,1)}, u32[]{:S(2)}) copy-start(bf16[512,1024]{1,0:T(8,128)(2,1)} %param.11) | copy-start | bytes 3145732
  6.5 4.7 %copy-start.14 = (f32[1024]{0:T(1024)S(1)}, f32[1024]{0:T(1024)}, u32[]{:S(2)}) copy-start(f32[1024]{0:T(1024)} %param.12) | copy-start | bytes 12292
  6.5 56.2 %all-gather.7.cloned.1.call-start = ((), (), s32[]{:S(2)}) async-start(), calls=%async_computation.1 | async-start | bytes 2359296 | tf_op jit(solution)/shard_map/all_gather | solution.py:106
  12.5 3.1 %copy-start.5 = (bf16[512,1024]{1,0:T(8,128)(2,1)S(1)}, bf16[512,1024]{1,0:T(8,128)(2,1)}, u32[]{:S(2)}) copy-start(bf16[512,1024]{1,0:T(8,128)(2,1)} %param.11) | copy-start | bytes 3145732
  12.5 3.1 %copy-start.8 = (bf16[1024,1024]{1,0:T(8,128)(2,1)S(1)}, bf16[1024,1024]{1,0:T(8,128)(2,1)}, u32[]{:S(2)}) copy-start(bf16[1024,1024]{1,0:T(8,128)(2,1)} %param.15) | copy-start | bytes 6291460
  15.6 1.4 copy-start.2
  17.0 4.2 %copy-start.13 = (s32[64,3]{0,1:T(4,128)S(1)}, s32[64,3]{0,1:T(4,128)}, u32[]{:S(2)}) copy-start(s32[64,3]{0,1:T(4,128)} %param.17) | copy-start | bytes 2308
  17.8 7.7 %collective-permute-start = (bf16[64,2048]{1,0:T(8,128)(2,1)}, bf16[64,2048]{1,0:T(8,128)(2,1)S(1)}, u32[]{:S(2)}, u32[]{:S(2)}) collective-permute-start(bf16[64,2048]{1,0:T(8,128)(2,1)} %get-tuple-element.98), channel_id=1, source_target_pairs={{0,4},{4,8},{8,12},{12,16},{16,20},{20,24},{24,28},{28,0},{1,5},{5... | collective-permute-start | bytes 786440 | tf_op jit(solution)/shard_map/ppermute | solution.py:19
  18.3 11.7 %collective-permute-start.1 = (bf16[64,2048]{1,0:T(8,128)(2,1)}, bf16[64,2048]{1,0:T(8,128)(2,1)}, u32[]{:S(2)}, u32[]{:S(2)}) collective-permute-start(bf16[64,2048]{1,0:T(8,128)(2,1)} %get-tuple-element.99), channel_id=1, source_target_pairs={{4,0},{8,4},{12,8},{16,12},{20,16},{24,20},{28,24},{0,28},{5,1},{9... | collective-permute-start | bytes 786440 | tf_op jit(solution)/shard_map/ppermute | solution.py:22
  42.8 94.8 %all-to-all-start = ((bf16[8,3,64,2048]{3,2,1,0:T(8,128)(2,1)}), bf16[8,3,64,2048]{3,2,1,0:T(8,128)(2,1)}, u32[]{:S(2)}, u32[]{:S(2)}) async-start(bf16[8,3,64,2048]{3,2,1,0:T(8,128)(2,1)} %bitcast.105), calls=%async_computation | async-start | bytes 12582912 | tf_op jit(solution)/shard_map/all_to_all | solution.py:92
  47.6 162.2 %all-gather.9.cloned.1.call-start = ((), (), s32[]{:S(2)}) async-start(), calls=%async_computation.2 | async-start | bytes 4718592 | tf_op jit(solution)/shard_map/all_gather | solution.py:28
  64.7 2.3 copy-start.7
  67.8 63.0 %copy-start.6 = (bf16[512,1024]{0,1:T(8,128)(2,1)S(1)}, bf16[512,1024]{0,1:T(8,128)(2,1)}, u32[]{:S(2)}) copy-start(bf16[512,1024]{0,1:T(8,128)(2,1)} %copy.51) | copy-start | bytes 3145732
  122.6 15.0 %copy-start.11 = (f32[128,128]{1,0:T(8,128)}, f32[128,128]{1,0:T(8,128)S(1)}, u32[]{:S(2)}) copy-start(f32[128,128]{1,0:T(8,128)S(1)} %all-gather.2) | copy-start | bytes 196612
  130.8 6.7 %copy-start.12 = (f32[128,128]{1,0:T(8,128)}, f32[128,128]{1,0:T(8,128)S(1)}, u32[]{:S(2)}) copy-start(f32[128,128]{1,0:T(8,128)S(1)} %all-gather.1) | copy-start | bytes 196612
  134.8 2.2 copy-start.9
  170.8 11.6 %copy-start.3 = (bf16[8,64,16,64]{3,2,1,0:T(8,128)(2,1)S(1)}, bf16[8,64,16,64]{3,2,1,0:T(8,128)(2,1)}, u32[]{:S(2)}) copy-start(bf16[8,64,16,64]{3,2,1,0:T(8,128)(2,1)} %reshape.283) | copy-start | bytes 3145732
  211.2 4.4 %slice-start = ((f32[128,128]{1,0:T(8,128)}), f32[16,128]{1,0:T(8,128)S(1)}, s32[]{:S(2)}) async-start(f32[128,128]{1,0:T(8,128)} %copy-done.11), calls=%async_computation.3 | async-start | bytes 16384 | tf_op jit(solution)/shard_map/slice | solution.py:29
  211.2 4.4 %slice-start.1 = ((f32[128,128]{1,0:T(8,128)}), f32[16,128]{1,0:T(8,128)S(1)}, s32[]{:S(2)}) async-start(f32[128,128]{1,0:T(8,128)} %copy-done.12), calls=%async_computation.4 | async-start | bytes 16384 | tf_op jit(solution)/shard_map/slice | solution.py:29
  232.6 1.2 copy-start.10
  233.0 5.1 %copy-start.1 = (bf16[1024,1024]{1,0:T(8,128)(2,1)S(1)}, bf16[1024,1024]{1,0:T(8,128)(2,1)}, u32[]{:S(2)}) copy-start(bf16[1024,1024]{1,0:T(8,128)(2,1)} %param.13) | copy-start | bytes 6291460
Sparse Core Ops, SparseCore 0:
  12.6 32.9 all-gather.6
  135.0 37.2 all-gather.8
